TPU v7x, 256 devices: a whole 4x4x8 slice. The times are simulated.
256 devices in a mesh: rows: 64 (over z, x, core), cols: 4 (over y).
Axes of the slice: x: 4, y: 4, z: 8, core: 2. Of those that a mesh axis runs over, the one named last changes fastest.
Arguments:
- front_rows: bfloat16 [8, 8192, 4096], P(None, 'rows', 'cols'), may hold values from -0.0625 to 0.0625
- heights: int32 [64, 8], P('rows'), may hold values from 1 to 128
- child_rows: bfloat16 [65536, 4096], P('rows', 'cols'), may hold values from -0.0625 to 0.0625
- child_dest: int32 [65536, 1], P('rows'), may hold values from 0 to 63; in each aligned block of 1024 rows (0 to 1023, 1024 to 2047, ...) at most 32 rows name the same one
- child_slot: int32 [65536], P('rows'), may hold values from 0 to 127
- parent_ids: int32 [1024], P('rows'), may hold values from 0 to 7
Outputs:
- r_rows: float32 [8, 128, 4096], P(None, None, ('cols', 'rows'))
Inputs may be any that keep to these rules, and one draw needn't show every extreme that they name: `child_dest`: in the rows of one device, at most 32 child rows name one index of rows.
All inputs are finite; a program needn't handle non-finite values.
Results may differ from a plain program's by a relative error of at most 0.002.
Values may be sent and summed in bfloat16 or wider, within the bound.
No kernel may reach another device: no remote copies, remote signals or barrier semaphores. Data moves between devices by JAX's collectives and lax.ppermute only.
A program may use at most 64 MiB of HBM per device.

v0:
```python
import jax
import jax.numpy as jnp
from jax import lax
from jax.sharding import PartitionSpec as P

NB = 128


def from_root(block, axis, holder):
    block = jnp.where(lax.axis_index(axis) == holder, block, jnp.zeros_like(block))
    return lax.psum(block, axis)


def solve_block(lower, columns):
    return jax.scipy.linalg.solve_triangular(lower, columns, lower=True)


def on_device(front_rows, heights, child_rows, child_dest, child_slot, parent_ids):
    fronts, height_cap, width = front_rows.shape
    peers = lax.axis_size("rows")
    child_count = child_rows.shape[0]
    capacity = max(2, 2 * child_count // peers)
    slots = peers * capacity
    destination = child_dest[:, 0]
    hits = (destination[:, None] == jnp.arange(peers, dtype=jnp.int32)[None, :]).astype(jnp.int32)
    before = jnp.cumsum(hits, axis=0) - hits
    position = jnp.sum(before * hits, axis=1)
    send_index = destination * capacity + position
    block_rows = child_count // parent_ids.shape[0]
    child_front = jnp.repeat(parent_ids, block_rows)
    send_rows = jnp.zeros((slots, width), jnp.bfloat16).at[send_index].set(child_rows)
    send_owner = jnp.zeros((slots,), jnp.int32).at[send_index].set(child_front)
    send_front = send_owner.astype(jnp.bfloat16)
    send_slot = (
        jnp.zeros((slots,), jnp.bfloat16).at[send_index].set(child_slot.astype(jnp.bfloat16))
    )
    live_mask = jnp.arange(height_cap, dtype=jnp.int32)[None, :] < heights[0][:, None]
    own = jnp.where(live_mask[:, :, None], front_rows, jnp.zeros_like(front_rows))
    got_rows, got_front, got_slot = (
        lax.all_to_all(
            send_rows.reshape(peers, capacity, width),
            "rows",
            split_axis=0,
            concat_axis=0,
            tiled=True,
        ),
        lax.all_to_all(
            send_front.reshape(peers, capacity), "rows", split_axis=0, concat_axis=0, tiled=True
        ),
        lax.all_to_all(
            send_slot.reshape(peers, capacity), "rows", split_axis=0, concat_axis=0, tiled=True
        ),
    )
    got_rows = got_rows.reshape(slots, width)
    got_lead = got_rows[:, :NB]
    target = got_front.reshape(-1).astype(jnp.int32) * height_cap + got_slot.reshape(-1).astype(
        jnp.int32
    )
    placing = (jnp.arange(fronts * height_cap, dtype=jnp.int32)[:, None] == target[None, :]).astype(
        jnp.bfloat16
    )
    added = jnp.dot(placing, got_lead, preferred_element_type=jnp.float32)
    panel_local = (
        own[:, :, :NB].reshape(fronts * height_cap, NB).astype(jnp.float32) + added
    ).astype(jnp.bfloat16)
    panel = from_root(panel_local.reshape(fronts, height_cap, NB), "cols", 0)
    selected = jnp.dot(
        placing.T, panel.reshape(fronts * height_cap, NB), preferred_element_type=jnp.float32
    ).astype(jnp.bfloat16)
    which = (
        jnp.arange(fronts, dtype=jnp.int32)[:, None]
        == got_front.reshape(-1).astype(jnp.int32)[None, :]
    ).astype(jnp.bfloat16)
    picked = which[:, :, None] * selected[None, :, :]
    child_cross = jnp.einsum("fsk,sc->fkc", picked, got_rows, preferred_element_type=jnp.float32)
    gram = jnp.einsum("fhk,fhj->fkj", panel, panel, preferred_element_type=jnp.float32)
    share_width = width // peers
    cross = jnp.einsum("fhk,fhc->fkc", panel, own, preferred_element_type=jnp.float32) + child_cross
    cross_total, gram_total = lax.psum((cross, gram), "rows")
    start = lax.axis_index("rows") * share_width
    columns = lax.dynamic_slice_in_dim(cross_total, start, share_width, 2)
    lower = jnp.linalg.cholesky(gram_total)
    return jax.vmap(solve_block)(lower, columns)


def solution(mesh):
    placed = (
        P(None, "rows", "cols"),
        P("rows", None),
        P("rows", "cols"),
        P("rows", None),
        P("rows"),
        P("rows"),
    )
    return jax.shard_map(
        on_device,
        mesh=mesh,
        in_specs=placed,
        out_specs=P(None, None, ("cols", "rows")),
        check_vma=False,
    )
```

profile of v0, /device:TPU:8, one launch (start us, length us, event | category | flops | bytes accessed | tf_op | source)
XLA Modules:
  0.0 623.2 jit_solution(7834299393505477574)
XLA Ops:
  6.5 0.7 fusion.21
  7.2 18.0 %reduce-window.6 = s32[64,8,128]{2,1,0:T(8,128)S(1)} reduce-window(s32[64,8,128]{2,1,0:T(8,128)S(1)} %fusion.21, s32[]{:T(128)} %constant.64.clone.1), window={size=1x1x128 pad=0_0x0_0x127_0}, to_apply=%region_0.0 | reduce-window | flops 8323072 | bytes 524292 | tf_op jit(solution)/shard_map/reduce-window
  25.4 0.1 copy.37
  25.7 0.1 broadcast_add_fusion
  25.8 0.8 fusion.20
  26.6 0.7 compare_select_fusion
  27.3 0.7 broadcast_in_dim.25
  28.1 4.3 scatter_custom_fusion
  32.4 0.7 all_to_all.20
  33.1 11.9 %all-to-all-start = ((bf16[64,1,32]{2,1,0:T(2,128)(2,1)}), bf16[64,1,32]{2,1,0:T(2,128)(2,1)S(1)}, u32[]{:S(2)}, u32[]{:S(2)}) async-start(bf16[64,1,32]{2,1,0:T(2,128)(2,1)} %all_to_all.20), calls=%async_computation | async-start | bytes 65536 | tf_op jit(solution)/shard_map/all_to_all | solution.py:47
  45.0 0.7 convert_element_type.64
  45.7 7.6 %scatter_custom_fusion.1 = bf16[2048]{0:T(1024)(128)(2,1)S(1)} fusion(s32[1024]{0:T(1024)S(1)} %bitcast.56, bf16[1024]{0:T(1024)(128)(2,1)S(1)} %convert_element_type.64, bf16[]{:T(256)} %constant.65.clone.1), kind=kCustom, calls=%fused_computation.48 | custom fusion | bytes 4098 | tf_op jit(solution)/shard_map/scatter | solution.py:35
  53.3 0.7 all_to_all.21
  54.0 0.6 all-to-all-done
  54.6 9.7 %all-to-all-start.1 = ((bf16[64,1,32]{2,1,0:T(2,128)(2,1)}), bf16[64,1,32]{2,1,0:T(2,128)(2,1)S(1)}, u32[]{:S(2)}, u32[]{:S(2)}) async-start(bf16[64,1,32]{2,1,0:T(2,128)(2,1)} %all_to_all.21), calls=%async_computation.1 | async-start | bytes 65536 | tf_op jit(solution)/shard_map/all_to_all | solution.py:50
  64.3 8.6 %scatter_custom_fusion.2 = bf16[2048,1024]{1,0:T(8,128)(2,1)} fusion(s32[1024]{0:T(1024)S(1)} %bitcast.57, bf16[1024,1024]{1,0:T(8,128)(2,1)} %param.8, bf16[]{:T(256)} %constant.65.clone.1), kind=kCustom, calls=%fused_computation.14 | custom fusion | bytes 4194816 | tf_op jit(solution)/shard_map/scatter | solution.py:31
  72.9 1.0 all-to-all-done.1
  73.9 9.7 %all-to-all-start.2 = ((bf16[64,32,1024]{2,1,0:T(8,128)(2,1)}), bf16[64,32,1024]{2,1,0:T(8,128)(2,1)}, u32[]{:S(2)}, u32[]{:S(2)}) async-start(bf16[64,32,1024]{2,1,0:T(8,128)(2,1)} %bitcast.46), calls=%async_computation.2 | async-start | bytes 8388608 | tf_op jit(solution)/shard_map/all_to_all | solution.py:40
  83.8 1.8 broadcast_select_fusion
  86.0 93.8 %all-to-all-done.2 = bf16[64,32,1024]{2,1,0:T(8,128)(2,1)} async-done(((bf16[64,32,1024]{2,1,0:T(8,128)(2,1)}), bf16[64,32,1024]{2,1,0:T(8,128)(2,1)}, u32[]{:S(2)}, u32[]{:S(2)}) %all-to-all-start.2) | async-done | bytes 4194336 | tf_op jit(solution)/shard_map/all_to_all | solution.py:40
  179.9 3.4 fusion.13
  183.4 42.1 %all-reduce.4.cloned.1.call-done = bf16[8,128,128]{2,1,0:T(8,128)(2,1)} async-done(((bf16[8,128,128]{2,1,0:T(8,128)(2,1)}), bf16[8,128,128]{2,1,0:T(8,128)(2,1)}) %all-reduce.4.cloned.1.call-update) | async-done | bytes 262160 | tf_op jit(solution)/shard_map/psum | solution.py:11
  225.5 3.3 fusion.6
  228.8 7.2 %fusion.2 = f32[8,128,1024]{1,2,0:T(8,128)S(1)} fusion(bf16[2048,1024,1]{1,0,2:T(8,128)(2,1)} %bitcast.15, bf16[2048,128]{1,0:T(8,128)(2,1)S(1)} %fusion.6, bf16[8,2048]{1,0:T(8,128)(2,1)S(1)} %fusion.23), kind=kOutput, calls=%fused_computation.6 | convolution fusion | flops 4297064448 | bytes 8945664 | tf_op jit(solution)/shard_map/fsk,sc->fkc/dot_general | solution.py:75
  236.1 1.1 fusion.29
  237.2 2.9 convolution_add_fusion
  240.1 198.9 %all-reduce.6.cloned.1.call-done = (f32[8,128,128]{1,2,0:T(8,128)}, f32[8,128,1024]{1,2,0:T(8,128)}) async-done(((f32[8,128,128]{1,2,0:T(8,128)}, f32[8,128,1024]{1,2,0:T(8,128)}), (f32[8,128,128]{1,2,0:T(8,128)}, f32[8,128,1024]{1,2,0:T(8,128)})) %all-reduce.6.cloned.1.call-update) | async-done | bytes 4718608 | tf_op jit(solution)/shard_map/psum | solution.py:79
  439.1 1.2 copy.43
  440.3 1.1 fusion.17
  441.4 94.0 %custom-call.8 = f32[8,128,128]{2,1,0:T(8,128)S(1)} custom-call(f32[8,128,128]{2,1,0:T(8,128)S(1)} %fusion.17), custom_call_target="Cholesky" | custom-call | tf_op jit(solution)/shard_map/jit(cholesky)/cholesky | solution.py:82
  535.7 78.6 %custom-call.9 = f32[8,1,128,128]{2,3,1,0:T(8,128)S(1)} custom-call(f32[8,1,128,128]{3,2,1,0:T(8,128)S(1)} %select_bitcast_fusion), custom_call_target="InvertDiagBlocksLowerTriangular" | custom-call | tf_op jit(solution)/shard_map/vmap(jit(_solve_triangular))/triangular_solve | solution.py:15
  614.3 2.0 fusion.15
  (27 shorter events, 1.3 us)
Async XLA Ops:
  33.1 21.6 %all-to-all-start = ((bf16[64,1,32]{2,1,0:T(2,128)(2,1)}), bf16[64,1,32]{2,1,0:T(2,128)(2,1)S(1)}, u32[]{:S(2)}, u32[]{:S(2)}) async-start(bf16[64,1,32]{2,1,0:T(2,128)(2,1)} %all_to_all.20), calls=%async_computation | async-start | bytes 65536 | tf_op jit(solution)/shard_map/all_to_all | solution.py:47
  54.6 19.2 %all-to-all-start.1 = ((bf16[64,1,32]{2,1,0:T(2,128)(2,1)}), bf16[64,1,32]{2,1,0:T(2,128)(2,1)S(1)}, u32[]{:S(2)}, u32[]{:S(2)}) async-start(bf16[64,1,32]{2,1,0:T(2,128)(2,1)} %all_to_all.21), calls=%async_computation.1 | async-start | bytes 65536 | tf_op jit(solution)/shard_map/all_to_all | solution.py:50
  73.9 9.8 %copy-start.1 = (s32[1,8]{1,0:T(1,128)S(1)}, s32[1,8]{1,0:T(1,128)}, u32[]{:S(2)}) copy-start(s32[1,8]{1,0:T(1,128)} %param.7) | copy-start | bytes 100
  73.9 106.0 %all-to-all-start.2 = ((bf16[64,32,1024]{2,1,0:T(8,128)(2,1)}), bf16[64,32,1024]{2,1,0:T(8,128)(2,1)}, u32[]{:S(2)}, u32[]{:S(2)}) async-start(bf16[64,32,1024]{2,1,0:T(8,128)(2,1)} %bitcast.46), calls=%async_computation.2 | async-start | bytes 8388608 | tf_op jit(solution)/shard_map/all_to_all | solution.py:40
  83.6 141.9 %all-reduce.4.cloned.1.call-start = ((), (), s32[]{:S(2)}) async-start(), calls=%async_computation.3 | async-start | bytes 524288 | tf_op jit(solution)/shard_map/psum | solution.py:11
  183.3 255.8 %all-reduce.6.cloned.1.call-start = ((), (), s32[]{:S(2)}) async-start(), calls=%async_computation.4 | async-start | bytes 9437184 | tf_op jit(solution)/shard_map/psum | solution.py:79
  228.8 7.3 %copy-start = (bf16[8,128,128]{2,1,0:T(8,128)(2,1)S(1)}, bf16[8,128,128]{2,1,0:T(8,128)(2,1)}, u32[]{:S(2)}) copy-start(bf16[8,128,128]{2,1,0:T(8,128)(2,1)} %all-reduce.4.cloned.1.call-done) | copy-start | bytes 786436
Sparse Core Ops, SparseCore 0:
  183.4 42.0 all-reduce.3
  240.2 198.7 all-reduce.5
where the time goes:
time: 624 us; the launch traced here: 623 us
  waiting for transfers between devices  336 us (54%)
  other arithmetic  197 us (32%)
  starting transfers between devices  31.4 us (5%)
  local copies, waits for them, and re-layouts  24.5 us (4%)
  matrix products  20 us (3%)
  between operations  13.6 us (2%)
    psum x1, waiting for transfers between devices, on_device(): cross_total, gram_total = lax.psum((cross, gram), 'rows')  199 us
    another operation x4, other arithmetic, on_device(): lower = jnp.linalg.cholesky(gram_total)  94.2 us
    all_to_all x1, waiting for transfers between devices, on_device(): lax.all_to_all(send_rows.reshape(peers, capacity, width), 'rows', split_a...  93.8 us
    another operation x3, other arithmetic, solve_block(): return jax.scipy.linalg.solve_triangular(lower, columns, lower=True)  78.7 us
    psum x1, waiting for transfers between devices, from_root(): return lax.psum(block, axis)  42.1 us
    another operation x3, other arithmetic  18.2 us
  transfers between devices with their start and end apart: 5, of which 5 were waited for; matrix products, arithmetic and copies ran while one was open for 3% of the time, Pallas kernels for 0%

commit v1 on v0

--- a/solution.py
+++ b/solution.py
@@ -8,7 +8,8 @@
 
 def from_root(block, axis, holder):
     block = jnp.where(lax.axis_index(axis) == holder, block, jnp.zeros_like(block))
-    return lax.psum(block, axis)
+    _move_lots_all = lambda s0, row_axis: jnp.sum(lax.all_gather(s0, row_axis), axis=0)
+    return _move_lots_all(block, axis)
 
 
 def solve_block(lower, columns):

time: 624 us -> 604 us (0.968)
  waiting for transfers between devices: 336 us -> 316 us
    psum x1 -> x0, waiting for transfers between devices: 42.1 us -> none  [from_root(): return lax.psum(block, axis)]
    all_gather x0 -> x1, waiting for transfers between devices: none -> 21.7 us  [from_root(): lax.all_gather(s0, row_axis)]
where the time goes in v1:
time: 604 us; the launch traced here: 603 us
  waiting for transfers between devices  316 us (52%)
  other arithmetic  199 us (33%)
  starting transfers between devices  31.4 us (5%)
  local copies, waits for them, and re-layouts  24.5 us (4%)
  matrix products  19 us (3%)
  between operations  13.6 us (2%)
    psum x1, waiting for transfers between devices, on_device(): cross_total, gram_total = lax.psum((cross, gram), 'rows')  199 us
    another operation x4, other arithmetic, on_device(): lower = jnp.linalg.cholesky(gram_total)  94.2 us
    all_to_all x1, waiting for transfers between devices, on_device(): lax.all_to_all(send_rows.reshape(peers, capacity, width), 'rows', split_a...  93.8 us
    another operation x3, other arithmetic, solve_block(): return jax.scipy.linalg.solve_triangular(lower, columns, lower=True)  78.7 us
    all_gather x1, waiting for transfers between devices, from_root(): lax.all_gather(s0, row_axis)  21.7 us
    another operation x3, other arithmetic  18.2 us
  transfers between devices with their start and end apart: 5, of which 5 were waited for; matrix products, arithmetic and copies ran while one was open for 3% of the time, Pallas kernels for 0%

profile of v1, /device:TPU:8, one launch (start us, length us, event | category | flops | bytes accessed | tf_op | source)
XLA Modules:
  0.0 603.1 jit_solution(8440931441772358067)
XLA Ops:
  6.5 0.7 fusion.21
  7.2 18.0 %reduce-window.6 = s32[64,8,128]{2,1,0:T(8,128)S(1)} reduce-window(s32[64,8,128]{2,1,0:T(8,128)S(1)} %fusion.21, s32[]{:T(128)} %constant.66.clone.1), window={size=1x1x128 pad=0_0x0_0x127_0}, to_apply=%region_0.0 | reduce-window | flops 8323072 | bytes 524292 | tf_op jit(solution)/shard_map/reduce-window
  25.4 0.1 copy.37
  25.8 0.8 fusion.20
  26.6 0.7 compare_select_fusion
  27.3 0.7 broadcast_in_dim.25
  28.1 4.3 scatter_custom_fusion
  32.4 0.7 all_to_all.20
  33.1 11.9 %all-to-all-start = ((bf16[64,1,32]{2,1,0:T(2,128)(2,1)}), bf16[64,1,32]{2,1,0:T(2,128)(2,1)S(1)}, u32[]{:S(2)}, u32[]{:S(2)}) async-start(bf16[64,1,32]{2,1,0:T(2,128)(2,1)} %all_to_all.20), calls=%async_computation | async-start | bytes 65536 | tf_op jit(solution)/shard_map/all_to_all | solution.py:48
  45.0 0.7 convert_element_type.66
  45.7 7.6 %scatter_custom_fusion.1 = bf16[2048]{0:T(1024)(128)(2,1)S(1)} fusion(s32[1024]{0:T(1024)S(1)} %bitcast.56, bf16[1024]{0:T(1024)(128)(2,1)S(1)} %convert_element_type.66, bf16[]{:T(256)} %constant.67.clone.1), kind=kCustom, calls=%fused_computation.48 | custom fusion | bytes 4098 | tf_op jit(solution)/shard_map/scatter | solution.py:36
  53.3 0.7 all_to_all.21
  54.0 0.6 all-to-all-done
  54.6 9.7 %all-to-all-start.1 = ((bf16[64,1,32]{2,1,0:T(2,128)(2,1)}), bf16[64,1,32]{2,1,0:T(2,128)(2,1)S(1)}, u32[]{:S(2)}, u32[]{:S(2)}) async-start(bf16[64,1,32]{2,1,0:T(2,128)(2,1)} %all_to_all.21), calls=%async_computation.1 | async-start | bytes 65536 | tf_op jit(solution)/shard_map/all_to_all | solution.py:51
  64.3 8.6 %scatter_custom_fusion.2 = bf16[2048,1024]{1,0:T(8,128)(2,1)} fusion(s32[1024]{0:T(1024)S(1)} %bitcast.57, bf16[1024,1024]{1,0:T(8,128)(2,1)} %param.8, bf16[]{:T(256)} %constant.67.clone.1), kind=kCustom, calls=%fused_computation.14 | custom fusion | bytes 4194816 | tf_op jit(solution)/shard_map/scatter | solution.py:32
  72.9 1.0 all-to-all-done.1
  73.9 9.7 %all-to-all-start.2 = ((bf16[64,32,1024]{2,1,0:T(8,128)(2,1)}), bf16[64,32,1024]{2,1,0:T(8,128)(2,1)}, u32[]{:S(2)}, u32[]{:S(2)}) async-start(bf16[64,32,1024]{2,1,0:T(8,128)(2,1)} %bitcast.46), calls=%async_computation.2 | async-start | bytes 8388608 | tf_op jit(solution)/shard_map/all_to_all | solution.py:41
  83.8 1.8 broadcast_select_fusion
  86.0 93.8 %all-to-all-done.2 = bf16[64,32,1024]{2,1,0:T(8,128)(2,1)} async-done(((bf16[64,32,1024]{2,1,0:T(8,128)(2,1)}), bf16[64,32,1024]{2,1,0:T(8,128)(2,1)}, u32[]{:S(2)}, u32[]{:S(2)}) %all-to-all-start.2) | async-done | bytes 4194336 | tf_op jit(solution)/shard_map/all_to_all | solution.py:41
  179.9 3.4 fusion.13
  183.4 21.7 %all-gather.2.cloned.1.call-done = bf16[4,8,128,128]{3,2,1,0:T(8,128)(2,1)} async-done(((bf16[1,8,128,128]{3,2,1,0:T(8,128)(2,1)}), bf16[4,8,128,128]{3,2,1,0:T(8,128)(2,1)}) %all-gather.2.cloned.1.call-update) | async-done | bytes 1048592 | tf_op jit(solution)/shard_map/all_gather | solution.py:11
  205.1 1.4 reduce_sum.25
  206.5 1.1 fusion.29
  207.6 2.4 fusion.6
  210.0 7.2 %fusion.2 = f32[8,128,1024]{1,2,0:T(8,128)S(1)} fusion(bf16[2048,1024,1]{1,0,2:T(8,128)(2,1)} %bitcast.15, bf16[2048,128]{1,0:T(8,128)(2,1)S(1)} %fusion.6, bf16[8,2048]{1,0:T(8,128)(2,1)S(1)} %fusion.23), kind=kOutput, calls=%fused_computation.6 | convolution fusion | flops 4297064448 | bytes 8945664 | tf_op jit(solution)/shard_map/fsk,sc->fkc/dot_general | solution.py:76
  217.2 2.9 convolution_add_fusion
  220.2 198.8 %all-reduce.3.cloned.1.call-done = (f32[8,128,128]{1,2,0:T(8,128)}, f32[8,128,1024]{1,2,0:T(8,128)}) async-done(((f32[8,128,128]{1,2,0:T(8,128)}, f32[8,128,1024]{1,2,0:T(8,128)}), (f32[8,128,128]{1,2,0:T(8,128)}, f32[8,128,1024]{1,2,0:T(8,128)})) %all-reduce.3.cloned.1.call-update) | async-done | bytes 4718608 | tf_op jit(solution)/shard_map/psum | solution.py:80
  419.0 1.2 copy.43
  420.2 1.1 fusion.17
  421.3 94.0 %custom-call.8 = f32[8,128,128]{2,1,0:T(8,128)S(1)} custom-call(f32[8,128,128]{2,1,0:T(8,128)S(1)} %fusion.17), custom_call_target="Cholesky" | custom-call | tf_op jit(solution)/shard_map/jit(cholesky)/cholesky | solution.py:83
  515.6 78.6 %custom-call.9 = f32[8,1,128,128]{2,3,1,0:T(8,128)S(1)} custom-call(f32[8,1,128,128]{3,2,1,0:T(8,128)S(1)} %select_bitcast_fusion), custom_call_target="InvertDiagBlocksLowerTriangular" | custom-call | tf_op jit(solution)/shard_map/vmap(jit(_solve_triangular))/triangular_solve | solution.py:16
  594.2 2.0 fusion.15
  (26 shorter events, 1.4 us)
Async XLA Ops:
  33.1 21.6 %all-to-all-start = ((bf16[64,1,32]{2,1,0:T(2,128)(2,1)}), bf16[64,1,32]{2,1,0:T(2,128)(2,1)S(1)}, u32[]{:S(2)}, u32[]{:S(2)}) async-start(bf16[64,1,32]{2,1,0:T(2,128)(2,1)} %all_to_all.20), calls=%async_computation | async-start | bytes 65536 | tf_op jit(solution)/shard_map/all_to_all | solution.py:48
  54.6 19.2 %all-to-all-start.1 = ((bf16[64,1,32]{2,1,0:T(2,128)(2,1)}), bf16[64,1,32]{2,1,0:T(2,128)(2,1)S(1)}, u32[]{:S(2)}, u32[]{:S(2)}) async-start(bf16[64,1,32]{2,1,0:T(2,128)(2,1)} %all_to_all.21), calls=%async_computation.1 | async-start | bytes 65536 | tf_op jit(solution)/shard_map/all_to_all | solution.py:51
  73.9 9.8 %copy-start = (s32[1,8]{1,0:T(1,128)S(1)}, s32[1,8]{1,0:T(1,128)}, u32[]{:S(2)}) copy-start(s32[1,8]{1,0:T(1,128)} %param.7) | copy-start | bytes 100
  73.9 106.0 %all-to-all-start.2 = ((bf16[64,32,1024]{2,1,0:T(8,128)(2,1)}), bf16[64,32,1024]{2,1,0:T(8,128)(2,1)}, u32[]{:S(2)}, u32[]{:S(2)}) async-start(bf16[64,32,1024]{2,1,0:T(8,128)(2,1)} %bitcast.46), calls=%async_computation.2 | async-start | bytes 8388608 | tf_op jit(solution)/shard_map/all_to_all | solution.py:41
  83.6 121.5 %all-gather.2.cloned.1.call-start = ((), (), s32[]{:S(2)}) async-start(), calls=%async_computation.3 | async-start | bytes 1310720 | tf_op jit(solution)/shard_map/all_gather | solution.py:11
  183.3 235.7 %all-reduce.3.cloned.1.call-start = ((), (), s32[]{:S(2)}) async-start(), calls=%async_computation.4 | async-start | bytes 9437184 | tf_op jit(solution)/shard_map/psum | solution.py:80
Sparse Core Ops, SparseCore 0:
  183.4 21.6 all-gather.1
  220.2 198.7 all-reduce.2
